TPU v7x, 256 devices: a whole 4x4x8 slice. The times are simulated.
256 devices in a mesh: rep: 8 (over x, z_hi), seq: 4 (over y), tp: 8 (over z_lo, core).
Axes of the slice: x: 4, y: 4, z: 8 (z_hi: 2, z_lo: 4; z = z_hi * 4 + z_lo), core: 2. Of those that a mesh axis runs over, the one named last changes fastest.
Arguments:
- hidden_in: bfloat16 [32768, 1536], P(('rep', 'seq', 'tp')), may hold values from -3 to 3
- routes: int32 [32768, 4], P(('rep', 'seq', 'tp')), may hold values from 0 to 31, all different within a row; in each aligned block of 128 rows (0 to 127, 128 to 255, ...) at most 24 rows name the same one
- prefix_len: int32 [8], replicated, may hold values from 256 to 2048, as said below
- cache: bfloat16 [8, 2, 2048, 256], P(None, None, ('rep', 'seq')), may hold values from -400 to 400, as said below
- attn_gain: float32 [1536], replicated, may hold values from 0.1 to 1.9
- w_query: bfloat16 [1536, 1024], P(None, 'tp'), may hold values from -0.375 to 0.375
- w_keyval: bfloat16 [2, 1536, 256], replicated, may hold values from -0.15625 to 0.15625
- w_out: bfloat16 [1024, 1536], P('tp'), may hold values from -0.375 to 0.375
- moe_gain: float32 [1536], replicated, may hold values from 0.1 to 1.9
- w_router: bfloat16 [1536, 32], replicated, may hold values from -0.15625 to 0.15625
- expert_in: bfloat16 [32, 1536, 1536], P(('seq', 'tp')), may hold values from -0.15625 to 0.15625
- expert_out: bfloat16 [32, 768, 1536], P(('seq', 'tp')), may hold values from -0.875 to 0.875
Outputs:
- hidden_out: bfloat16 [32768, 1536], P(('rep', 'seq', 'tp'))
- new_cache: bfloat16 [32768, 512], P(('rep', 'seq'), 'tp')
Inputs may be any that keep to these rules, and one draw needn't show every extreme that they name: `routes`: each row names 4 different experts; within the rows of one device (aligned blocks of 128 rows) no expert is named by more than 24 rows. prefix_len[r] cached positions (0 to prefix_len[r] - 1) of request r are valid; some request has 2048. cache[r, g, p, 0:128] is a key, cache[r, g, p, 128:] a value.
All inputs are finite; a program needn't handle non-finite values.
Results may differ from a plain program's by a relative error of at most 0.029.
The roundings to bfloat16 on the way count: a program that leaves them out, or rounds other values in their place, can miss the bound.
Values may be sent and summed in bfloat16 or wider, within the bound.
No kernel may reach another device: no remote copies, remote signals or barrier semaphores. Data moves between devices by JAX's collectives and lax.ppermute only.
A program may use at most 64 MiB of HBM per device.

v0:
```python
import jax
import jax.numpy as jnp
from jax import lax
from jax.sharding import PartitionSpec as P

CAP = 24
epsilon = 1e-06
masked_score = -1e30


def rms_scale(rows, gain):
    values = rows.astype(jnp.float32)
    inverse = lax.rsqrt(jnp.mean(values * values, axis=-1, keepdims=True) + epsilon)
    return (values * inverse * gain).astype(jnp.bfloat16)


def attend(state, query_rows, block, visible, scale):
    best, total, summed = state
    head_dim = block.shape[1] // 2
    scores = (
        lax.dot_general(
            query_rows,
            block[:, :head_dim],
            (((1,), (1,)), ((), ())),
            preferred_element_type=jnp.float32,
        )
        * scale
    )
    scores = jnp.where(visible, scores, masked_score)
    new_best = jnp.maximum(best, jnp.max(scores, axis=1))
    weights = jnp.where(visible, jnp.exp(scores - new_best[:, None]), 0.0)
    factor = jnp.exp(best - new_best)
    total = total * factor + jnp.sum(weights, axis=1)
    summed = summed * factor[:, None] + jnp.dot(
        weights.astype(jnp.bfloat16), block[:, head_dim:], preferred_element_type=jnp.float32
    )
    return (new_best, total, summed)


def body(
    hidden_in,
    routes,
    prefix_len,
    cache,
    attn_gain,
    w_query,
    w_keyval,
    w_out,
    moe_gain,
    w_router,
    expert_in,
    expert_out,
):
    tp_count = lax.axis_size("tp")
    seq_count = lax.axis_size("seq")
    rep_count = lax.axis_size("rep")
    tp_index = lax.axis_index("tp")
    seq_index = lax.axis_index("seq")
    rep_index = lax.axis_index("rep")
    rows_dev, width = hidden_in.shape
    kv_heads = w_keyval.shape[0]
    pair_cols = w_keyval.shape[2]
    head_dim = pair_cols // 2
    query_cols = w_query.shape[1]
    heads_dev = query_cols // head_dim
    piece_len = rows_dev * tp_count
    scale = 1.0 / float(head_dim) ** 0.5
    kv_index = tp_index // (tp_count // kv_heads)
    normed = rms_scale(hidden_in, attn_gain)
    head_weight = lax.dynamic_index_in_dim(w_keyval, kv_index, 0, keepdims=False)
    joined = jnp.concatenate([w_query, head_weight], axis=1)
    projected = jnp.dot(
        lax.all_gather(normed, "tp", axis=0, tiled=True), joined, preferred_element_type=jnp.float32
    ).astype(jnp.bfloat16)
    count_rows = piece_len * heads_dev
    query_rows = projected[:, :query_cols]
    fresh = projected[:, query_cols:]
    col_width = kv_heads * pair_cols // tp_count
    new_cache = lax.dynamic_slice_in_dim(fresh, tp_index * col_width % pair_cols, col_width, 1)
    own_pages = lax.dynamic_index_in_dim(cache, kv_index, 1, keepdims=True)
    fetched = lax.all_to_all(own_pages, "rep", split_axis=0, concat_axis=2, tiled=True)
    page_rows = fetched.shape[2]
    pages = fetched.reshape(page_rows, pair_cols)
    page_len = page_rows // rep_count
    length = lax.dynamic_index_in_dim(prefix_len, rep_index, 0, keepdims=False)
    row_ids = jnp.arange(page_rows, dtype=jnp.int32)

    def page_visible(source):
        position = (row_ids // page_len * seq_count + source) * page_len + row_ids % page_len
        return (position < length)[None, :]

    def fresh_visible(source, query_piece):
        token = jnp.arange(count_rows, dtype=jnp.int32) // heads_dev + query_piece * piece_len
        key_pos = source * piece_len + jnp.arange(piece_len, dtype=jnp.int32)
        return key_pos[None, :] <= token[:, None]

    start_state = (
        jnp.full((count_rows,), masked_score, jnp.float32),
        jnp.zeros((count_rows,), jnp.float32),
        jnp.zeros((count_rows, head_dim), jnp.float32),
    )
    shard_rows = page_rows + piece_len
    local_keys = jnp.concatenate([pages, fresh], axis=0)

    def fold_shard(state, shard, source):
        state = attend(state, query_rows, shard[:page_rows], page_visible(source), scale)

        def with_fresh(inner):
            return attend(
                inner, query_rows, shard[page_rows:], fresh_visible(source, seq_index), scale
            )

        return lax.cond(source <= seq_index, with_fresh, lambda inner: inner, state)

    state = start_state
    gathered = lax.all_gather(local_keys, "seq", axis=0, tiled=True)
    count = gathered.shape[0] // shard_rows
    shards = gathered.reshape(count, shard_rows, pair_cols)

    def advance(inner, item):
        offset, shard = item
        return (fold_shard(inner, shard, offset), None)

    state, _ = lax.scan(advance, state, (jnp.arange(count, dtype=jnp.int32), shards))
    best, total, summed = state
    attended = (summed / total[:, None]).astype(jnp.bfloat16)
    rows = attended
    head_total = lax.psum_scatter(
        jnp.dot(rows, w_out, preferred_element_type=jnp.float32),
        "tp",
        scatter_dimension=0,
        tiled=True,
    )
    mid = (hidden_in.astype(jnp.float32) + head_total).astype(jnp.bfloat16)
    normed_moe = rms_scale(mid, moe_gain)
    experts_all = w_router.shape[1]
    top = routes.shape[1]
    expert_ids = jnp.arange(experts_all, dtype=jnp.int32)
    logits = jnp.dot(normed_moe, w_router, preferred_element_type=jnp.float32)
    matches = routes[:, :, None] == expert_ids[None, None, :]
    chosen = jnp.sum(jnp.where(matches, logits[:, None, :], 0.0), axis=2)
    raised = jnp.exp(chosen)
    gates = raised / jnp.sum(raised, axis=1, keepdims=True)
    flat_routes = routes.reshape(rows_dev * top)
    onehot = (flat_routes[:, None] == expert_ids[None, :]).astype(jnp.int32)
    before = jnp.cumsum(onehot, axis=0) - onehot
    slot = jnp.sum(before * onehot, axis=1)
    target = flat_routes * CAP + slot
    outgoing = (
        jnp.zeros((experts_all * CAP, width), jnp.bfloat16)
        .at[target]
        .set(jnp.repeat(normed_moe, top, axis=0))
    )
    group_count = seq_count * tp_count
    local_experts = expert_in.shape[0]
    inner_dim = expert_out.shape[1]
    arrived = lax.all_to_all(
        outgoing.reshape(group_count, local_experts, CAP, width),
        ("seq", "tp"),
        split_axis=0,
        concat_axis=0,
        tiled=True,
    )
    rows = arrived[:, 0].reshape(-1, width)
    inner = jnp.dot(rows, expert_in[0], preferred_element_type=jnp.float32)
    active = (jnp.maximum(inner[:, :inner_dim], 0.0) * inner[:, inner_dim:]).astype(jnp.bfloat16)
    output = jnp.dot(active, expert_out[0], preferred_element_type=jnp.float32).astype(jnp.bfloat16)
    results = [output.reshape(arrived.shape[0], arrived.shape[2], width)]
    returned = lax.all_to_all(
        jnp.stack(results, axis=1), ("seq", "tp"), split_axis=0, concat_axis=0, tiled=True
    )
    picked = returned.reshape(experts_all * CAP, width)[target].reshape(rows_dev, top, width)
    mixed = jnp.sum(gates[:, :, None] * picked.astype(jnp.float32), axis=1)
    hidden_out = (mid.astype(jnp.float32) + mixed).astype(jnp.bfloat16)
    return (hidden_out, new_cache)


def solution(mesh):
    placed = (
        P(("rep", "seq", "tp"), None),
        P(("rep", "seq", "tp"), None),
        P(),
        P(None, None, ("rep", "seq"), None),
        P(),
        P(None, "tp"),
        P(),
        P("tp", None),
        P(),
        P(),
        P(("seq", "tp"), None, None),
        P(("seq", "tp"), None, None),
    )
    return jax.shard_map(
        body,
        mesh=mesh,
        in_specs=placed,
        out_specs=(P(("rep", "seq", "tp"), None), P(("rep", "seq"), "tp")),
        check_vma=False,
    )
```

profile of v0, /device:TPU:1, one launch (start us, length us, event | category | flops | bytes accessed | tf_op | source)
XLA Modules:
  0.0 418.8 jit_solution(9488731846069213498)
XLA Ops:
  7.2 1.3 fusion.57
  8.6 1.9 fusion.59
  10.5 1.7 constant_dynamic-slice_fusion.2
  12.2 11.5 %all-to-all-start = ((bf16[8,1,64,256]{3,2,1,0:T(8,128)(2,1)}), bf16[8,1,64,256]{3,2,1,0:T(8,128)(2,1)S(1)}, u32[]{:S(2)}, u32[]{:S(2)}) async-start(bf16[8,1,64,256]{3,2,1,0:T(8,128)(2,1)} %constant_dynamic-slice_fusion.2), calls=%async_computation | async-start | bytes 524288 | tf_op jit(solution)/shard_map/all_to_all | solution.py:81
  23.7 2.1 dynamic-slice_bitcast_fusion.1
  25.8 8.2 %all-to-all-done = bf16[8,1,64,256]{3,2,1,0:T(8,128)(2,1)S(1)} async-done(((bf16[8,1,64,256]{3,2,1,0:T(8,128)(2,1)}), bf16[8,1,64,256]{3,2,1,0:T(8,128)(2,1)S(1)}, u32[]{:S(2)}, u32[]{:S(2)}) %all-to-all-start) | async-done | bytes 262176 | tf_op jit(solution)/shard_map/all_to_all | solution.py:81
  34.2 26.8 %all-gather.3.cloned.1.call-done = bf16[1024,1536]{1,0:T(8,128)(2,1)} async-done(((bf16[128,1536]{1,0:T(8,128)(2,1)}), bf16[1024,1536]{1,0:T(8,128)(2,1)}) %all-gather.3.cloned.1.call-update) | async-done | bytes 3145744 | tf_op jit(solution)/shard_map/all_gather | solution.py:73
  61.0 3.5 convolution_convert_fusion.1
  69.2 41.3 %all-gather.5.cloned.1.call-done = bf16[6144,256]{0,1:T(8,128)(2,1)} async-done(((bf16[1536,256]{0,1:T(8,128)(2,1)}), bf16[6144,256]{0,1:T(8,128)(2,1)}) %all-gather.5.cloned.1.call-update) | async-done | bytes 3145744 | tf_op jit(solution)/shard_map/all_gather | solution.py:116
  110.6 4.6 %copy.48 = bf16[6144,256]{1,0:T(8,128)(2,1)} copy(bf16[6144,256]{0,1:T(8,128)(2,1)} %all-gather.5.cloned.1.call-done) | data formatting | bytes 6291456
  116.0 39.8 %while.20 = (s32[]{:T(128)}, f32[1024]{0:T(1024)S(1)}, f32[1024]{0:T(1024)S(1)}, f32[1024,128]{1,0:T(8,128)}, s32[4]{0:T(128)S(1)}, /*index=5*/s32[]{:T(128)}, s...) while((s32[]{:T(128)}, f32[1024]{0:T(1024)S(1)}, ...), condition=%wide.region_8.9_spmd.clone.clone, body=%wide.region_1.8_spmd.clone.clone.sunk | while | flops 829438464 | bytes 24546600 | solution.py:124
  121.7 2.7 convolution_add_fusion.2
  124.4 6.2 %conditional.4 = ((f32[1024]{0:T(1024)S(1)}, f32[1024]{0:T(1024)S(1)}, f32[1024,128]{1,0:T(8,128)})) conditional(s32[]{:T(128)} %convert_element_type.129, (f32[1024]{0:T(1024)S(1)}, f32[1024]{0:T(1024)S(1)}, f32[1024,128]{1,0:T(8,128)}) %tuple.70, (s32[]{:T(128)}, s32[]{:T(128)}, bf16[1,1536,256]{2,1,0:T(8,128)(2,1)S(1)}, ...), branch_computations={%region_4.4_spmd, %region_5.7_spmd} | conditional | flops 553914368 | bytes 14516288 | solution.py:113
  125.8 1.5 fusion.10
  127.4 3.3 fusion.13
  136.3 2.7 convolution_add_fusion.2
  144.7 2.7 convolution_add_fusion.2
  153.1 2.7 convolution_add_fusion.2
  155.8 4.8 %fusion.65 = f32[1024,1536]{1,0:T(8,128)} fusion(bf16[128,1536]{1,0:T(8,128)(2,1)} %param.23, f32[1024,128]{1,0:T(8,128)} %get-tuple-element.277, f32[1024]{0:T(1024)S(1)} %get-tuple-element.278), kind=kOutput, calls=%fused_computation.89 | convolution fusion | flops 402915328 | bytes 7213056 | tf_op jit(solution)/shard_map/dot_general | solution.py:129
  163.5 87.9 %reduce-scatter.2.cloned.1.call-done = f32[128,1536]{1,0:T(8,128)} async-done(((f32[1024,1536]{1,0:T(8,128)}), f32[128,1536]{1,0:T(8,128)}) %reduce-scatter.2.cloned.1.call-update) | async-done | bytes 786448 | tf_op jit(solution)/shard_map/reduce_scatter | solution.py:128
  253.0 1.6 broadcast_in_dim.96
  254.5 3.7 reshape.208
  258.2 5.5 %scatter_custom_fusion = bf16[768,1536]{1,0:T(8,128)(2,1)} fusion(s32[512]{0:T(512)S(1)} %bitcast.64, bf16[512,1536]{1,0:T(8,128)(2,1)} %reshape.208, bf16[]{:T(256)} %constant.204.clone.1), kind=kCustom, calls=%fused_computation.76 | custom fusion | bytes 2359808 | tf_op jit(solution)/shard_map/scatter | solution.py:152
  263.8 63.9 %all_to_all.19 = bf16[32,1,24,1536]{3,2,1,0:T(8,128)(2,1)S(1)} all-to-all(bf16[32,1,24,1536]{3,2,1,0:T(8,128)(2,1)} %bitcast.60), channel_id=1, replica_groups=mesh['rep'=8,'seq'=4,'tp'=8] {'seq','tp'}, dimensions={0} | all-to-all | bytes 4718592 | tf_op jit(solution)/shard_map/all_to_all | solution.py:157
  327.7 5.7 %fusion.46 = f32[768,1536]{1,0:T(8,128)S(1)} fusion(bf16[768,1536]{1,0:T(8,128)(2,1)S(1)} %bitcast.62, bf16[1,1536,1536]{2,1,0:T(8,128)(2,1)} %param.26), kind=kOutput, calls=%fused_computation.57 | convolution fusion | flops 3623878656 | bytes 11796480 | tf_op jit(solution)/shard_map/dot_general | solution.py:165
  333.4 3.4 convolution_convert_fusion
  336.7 4.7 %all-to-all-start.2 = ((bf16[32,1,24,1536]{3,2,1,0:T(8,128)(2,1)}), bf16[32,1,24,1536]{3,2,1,0:T(8,128)(2,1)}, u32[]{:S(2)}, u32[]{:S(2)}) async-start(bf16[32,1,24,1536]{3,2,1,0:T(8,128)(2,1)} %bitcast.61), calls=%async_computation.3 | async-start | bytes 4718592 | tf_op jit(solution)/shard_map/all_to_all | solution.py:169
  341.5 1.6 constant_dynamic-slice_fusion.1
  343.5 53.2 %all-to-all-done.2 = bf16[32,1,24,1536]{3,2,1,0:T(8,128)(2,1)} async-done(((bf16[32,1,24,1536]{3,2,1,0:T(8,128)(2,1)}), bf16[32,1,24,1536]{3,2,1,0:T(8,128)(2,1)}, u32[]{:S(2)}, u32[]{:S(2)}) %all-to-all-start.2) | async-done | bytes 2359328 | tf_op jit(solution)/shard_map/all_to_all | solution.py:169
  396.7 6.4 %gather_fusion = bf16[512,1536]{1,0:T(8,128)(2,1)} fusion(bf16[768,1536]{1,0:T(8,128)(2,1)} %bitcast.14, s32[1024]{0:T(1024)S(1)} %pad_clamp_fusion), kind=kCustom, calls=%fused_computation | custom fusion | bytes 3147776 | tf_op jit(solution)/shard_map/gather | solution.py:172
  403.1 4.2 %reshape.195 = f32[128,4,1536]{2,1,0:T(4,128)} reshape(bf16[512,1536]{1,0:T(8,128)(2,1)} %gather_fusion) | data formatting | bytes 4718592 | tf_op jit(solution)/shard_map/convert_element_type | solution.py:173
  407.3 4.2 multiply_reduce_fusion
  (106 shorter events, 32.4 us)
Async XLA Ops:
  7.2 326.2 %copy-start = (bf16[1,768,1536]{2,1,0:T(8,128)(2,1)S(1)}, bf16[1,768,1536]{2,1,0:T(8,128)(2,1)}, u32[]{:S(2)}) copy-start(bf16[1,768,1536]{2,1,0:T(8,128)(2,1)} %param.27) | copy-start | bytes 7077892
  7.2 53.8 %copy-start.7 = (bf16[1536,128]{1,0:T(8,128)(2,1)S(1)}, bf16[1536,128]{1,0:T(8,128)(2,1)}, u32[]{:S(2)}) copy-start(bf16[1536,128]{1,0:T(8,128)(2,1)} %param.21) | copy-start | bytes 1179652
  7.2 53.8 %all-gather.3.cloned.1.call-start = ((), (), s32[]{:S(2)}) async-start(), calls=%async_computation.4 | async-start | bytes 3538944 | tf_op jit(solution)/shard_map/all_gather | solution.py:73
  12.2 21.8 %all-to-all-start = ((bf16[8,1,64,256]{3,2,1,0:T(8,128)(2,1)}), bf16[8,1,64,256]{3,2,1,0:T(8,128)(2,1)S(1)}, u32[]{:S(2)}, u32[]{:S(2)}) async-start(bf16[8,1,64,256]{3,2,1,0:T(8,128)(2,1)} %constant_dynamic-slice_fusion.2), calls=%async_computation | async-start | bytes 524288 | tf_op jit(solution)/shard_map/all_to_all | solution.py:81
  23.7 86.9 %all-gather.5.cloned.1.call-start = ((), (), s32[]{:S(2)}) async-start(), calls=%async_computation.5 | async-start | bytes 3932160 | tf_op jit(solution)/shard_map/all_gather | solution.py:116
  64.5 0.9 copy-start.3
  65.4 2.1 copy-start.8
  65.4 0.8 copy-start.2
  67.2 184.3 %reduce-scatter.2.cloned.1.call-start = ((), (), s32[]{:S(2)}) async-start(), calls=%async_computation.6 | async-start | bytes 7077888 | tf_op jit(solution)/shard_map/reduce_scatter | solution.py:128
  160.7 0.7 copy-start.5
  160.7 90.8 %copy-start.1 = (bf16[128,1536]{1,0:T(8,128)(2,1)S(1)}, bf16[128,1536]{1,0:T(8,128)(2,1)}, u32[]{:S(2)}) copy-start(bf16[128,1536]{1,0:T(8,128)(2,1)} %param.16) | copy-start | bytes 1179652
  160.7 92.1 %copy-start.6 = (f32[1536]{0:T(1024)S(1)}, f32[1536]{0:T(1024)}, u32[]{:S(2)}) copy-start(f32[1536]{0:T(1024)} %param.24) | copy-start | bytes 18436
  336.7 6.3 %copy-start.4 = (bf16[1536,32]{0,1:T(8,128)(2,1)S(1)}, bf16[1536,32]{0,1:T(8,128)(2,1)}, u32[]{:S(2)}) copy-start(bf16[1536,32]{0,1:T(8,128)(2,1)} %param.25) | copy-start | bytes 294916
  336.7 60.0 %all-to-all-start.2 = ((bf16[32,1,24,1536]{3,2,1,0:T(8,128)(2,1)}), bf16[32,1,24,1536]{3,2,1,0:T(8,128)(2,1)}, u32[]{:S(2)}, u32[]{:S(2)}) async-start(bf16[32,1,24,1536]{3,2,1,0:T(8,128)(2,1)} %bitcast.61), calls=%async_computation.3 | async-start | bytes 4718592 | tf_op jit(solution)/shard_map/all_to_all | solution.py:169
Sparse Core Ops, SparseCore 0:
  10.6 50.3 all-gather.2
  67.3 43.2 all-gather.4
  160.8 90.5 reduce-scatter.1
where the time goes:
time: 421 us; the launch traced here: 419 us
  waiting for transfers between devices  218 us (52%)
  blocking collectives  63.9 us (15%)
  local copies, waits for them, and re-layouts  48.4 us (11%)
  matrix products  34.3 us (8%)
  other arithmetic  21.2 us (5%)
  starting transfers between devices  16.5 us (4%)
  between operations  14 us (3%)
    reduce_scatter x1, waiting for transfers between devices, body(): lax.psum_scatter(jnp.dot(rows, w_out, preferred_element_type=jnp.float32)...  87.9 us
    all_to_all x1, blocking collectives, body(): lax.all_to_all(outgoing.reshape(group_count, local_experts, CAP, width),...  63.9 us
    all_to_all x1, waiting for transfers between devices, body(): lax.all_to_all(jnp.stack(results, axis=1), ('seq', 'tp'), split_axis=0, c...  53.2 us
    all_gather x1, waiting for transfers between devices, body(): gathered = lax.all_gather(local_keys, 'seq', axis=0, tiled=True)  41.3 us
    all_gather x1, waiting for transfers between devices, body(): lax.all_gather(normed, 'tp', axis=0, tiled=True)  26.8 us
    dot_general x5, matrix products, attend(): jnp.dot(weights.astype(jnp.bfloat16), block[:, head_dim:], preferred_elem...  14.1 us
    all_to_all x1, starting transfers between devices, body(): lax.all_to_all(own_pages, 'rep', split_axis=0, concat_axis=2, tiled=True)  11.5 us
  transfers between devices with their start and end apart: 5, of which 5 were waited for; matrix products, arithmetic and copies ran while one was open for 2% of the time, Pallas kernels for 0%

commit v1 on v0

--- a/solution.py
+++ b/solution.py
@@ -113,7 +113,22 @@
         return lax.cond(source <= seq_index, with_fresh, lambda inner: inner, state)
 
     state = start_state
-    gathered = lax.all_gather(local_keys, "seq", axis=0, tiled=True)
+    ways, here, step = (lax.axis_size("seq"), lax.axis_index("seq"), local_keys.shape[0])
+    dims = [n * ways if d == 0 else n for d, n in enumerate(local_keys.shape)]
+    gathered = lax.dynamic_update_slice_in_dim(
+        jnp.zeros(dims, local_keys.dtype), local_keys, here * step, axis=0
+    )
+    going_up = going_down = local_keys
+    for far in range(1, ways // 2 + 1):
+        going_up = lax.ppermute(going_up, "seq", [(d, (d + 1) % ways) for d in range(ways)])
+        gathered = lax.dynamic_update_slice_in_dim(
+            gathered, going_up, (here - far) % ways * step, axis=0
+        )
+        if 2 * far < ways:
+            going_down = lax.ppermute(going_down, "seq", [(d, (d - 1) % ways) for d in range(ways)])
+            gathered = lax.dynamic_update_slice_in_dim(
+                gathered, going_down, (here + far) % ways * step, axis=0
+            )
     count = gathered.shape[0] // shard_rows
     shards = gathered.reshape(count, shard_rows, pair_cols)
 

time: 421 us -> 414 us (0.983)
  waiting for transfers between devices: 218 us -> 200 us
  local copies, waits for them, and re-layouts: 48.4 us -> 56.6 us
    all_gather x1 -> x0, waiting for transfers between devices: 41.3 us -> none  [body(): gathered = lax.all_gather(local_keys, 'seq', axis=0, tiled=True)]
    ppermute x0 -> x3, waiting for transfers between devices: none -> 19.8 us  [the longest x2 19.8 us: body(): lax.ppermute(going_up, 'seq', [(d, (d + 1) % ways) for d in range(ways)])]
    unnamed x21 -> x22, local copies, waits for them, and re-layouts: 7.26 us -> 1.92 us
    ppermute x0 -> x3, local copies, waits for them, and re-layouts: none -> 5.15 us  [the longest x2 3.75 us: body(): lax.ppermute(going_up, 'seq', [(d, (d + 1) % ways) for d in range(ways)])]
    dynamic_update_slice x0 -> x4, local copies, waits for them, and re-layouts: none -> 4.92 us  [the longest x2 3.03 us: body(): lax.dynamic_update_slice_in_dim(gathered, going_up, (here - far) % ways *...]
  transfers between devices with their start and end apart: 5 -> 7, of which waited for: 5 -> 6; matrix products, arithmetic and copies ran while one was open for 2% -> 5% of each run, Pallas kernels for 0% -> 0%
where the time goes in v1:
time: 414 us; the launch traced here: 412 us
  waiting for transfers between devices  200 us (48%)
  blocking collectives  63.9 us (15%)
  local copies, waits for them, and re-layouts  56.6 us (14%)
  matrix products  34.2 us (8%)
  other arithmetic  20.1 us (5%)
  starting transfers between devices  19.5 us (5%)
  between operations  14.3 us (3%)
    reduce_scatter x1, waiting for transfers between devices, body(): lax.psum_scatter(jnp.dot(rows, w_out, preferred_element_type=jnp.float32)...  92 us
    all_to_all x1, blocking collectives, body(): lax.all_to_all(outgoing.reshape(group_count, local_experts, CAP, width),...  63.9 us
    all_to_all x1, waiting for transfers between devices, body(): lax.all_to_all(jnp.stack(results, axis=1), ('seq', 'tp'), split_axis=0, c...  53.2 us
    all_gather x1, waiting for transfers between devices, body(): lax.all_gather(normed, 'tp', axis=0, tiled=True)  26.1 us
    ppermute x2, waiting for transfers between devices, body(): lax.ppermute(going_up, 'seq', [(d, (d + 1) % ways) for d in range(ways)])  19.8 us
    dot_general x5, matrix products, attend(): jnp.dot(weights.astype(jnp.bfloat16), block[:, head_dim:], preferred_elem...  14.1 us
    all_to_all x1, starting transfers between devices, body(): lax.all_to_all(own_pages, 'rep', split_axis=0, concat_axis=2, tiled=True)  11.5 us
    all_to_all x1, waiting for transfers between devices, body(): lax.all_to_all(own_pages, 'rep', split_axis=0, concat_axis=2, tiled=True)  9.09 us
  transfers between devices with their start and end apart: 7, of which 6 were waited for; matrix products, arithmetic and copies ran while one was open for 5% of the time, Pallas kernels for 0%

profile of v1, /device:TPU:1, one launch (start us, length us, event | category | flops | bytes accessed | tf_op | source)
XLA Modules:
  0.0 412.4 jit_solution(2827620236190262105)
XLA Ops:
  8.5 1.9 fusion.59
  10.5 1.7 constant_dynamic-slice_fusion.2
  12.2 11.5 %all-to-all-start = ((bf16[8,1,64,256]{3,2,1,0:T(8,128)(2,1)}), bf16[8,1,64,256]{3,2,1,0:T(8,128)(2,1)S(1)}, u32[]{:S(2)}, u32[]{:S(2)}) async-start(bf16[8,1,64,256]{3,2,1,0:T(8,128)(2,1)} %constant_dynamic-slice_fusion.2), calls=%async_computation | async-start | bytes 524288 | tf_op jit(solution)/shard_map/all_to_all | solution.py:81
  24.9 9.1 %all-to-all-done = bf16[8,1,64,256]{3,2,1,0:T(8,128)(2,1)S(1)} async-done(((bf16[8,1,64,256]{3,2,1,0:T(8,128)(2,1)}), bf16[8,1,64,256]{3,2,1,0:T(8,128)(2,1)S(1)}, u32[]{:S(2)}, u32[]{:S(2)}) %all-to-all-start) | async-done | bytes 262176 | tf_op jit(solution)/shard_map/all_to_all | solution.py:81
  34.9 26.1 %all-gather.2.cloned.1.call-done = bf16[1024,1536]{1,0:T(8,128)(2,1)} async-done(((bf16[128,1536]{1,0:T(8,128)(2,1)}), bf16[1024,1536]{1,0:T(8,128)(2,1)}) %all-gather.2.cloned.1.call-update) | async-done | bytes 3145744 | tf_op jit(solution)/shard_map/all_gather | solution.py:73
  61.0 3.4 convolution_convert_fusion.1
  64.5 1.6 collective-permute-start
  67.6 16.0 %collective-permute-done = bf16[1536,256]{0,1:T(8,128)(2,1)} collective-permute-done((bf16[1536,256]{0,1:T(8,128)(2,1)S(1)}, bf16[1536,256]{0,1:T(8,128)(2,1)}, u32[]{:S(2)}, u32[]{:S(2)}) %collective-permute-start) | collective-permute-done | bytes 786464 | tf_op jit(solution)/shard_map/ppermute | solution.py:123
  85.5 1.7 slice.75
  88.3 1.9 broadcast_in_dim.96
  91.1 2.3 copy.50
  94.9 2.1 constant_dynamic-update-slice_fusion.2
  97.9 3.8 collective-permute-done.2
  104.9 40.1 %while.20 = (s32[]{:T(128)}, f32[1024]{0:T(1024)S(1)}, f32[1024]{0:T(1024)S(1)}, f32[1024,128]{1,0:T(8,128)}, s32[4]{0:T(128)S(1)}, /*index=5*/s32[]{:T(128)}, s...) while((s32[]{:T(128)}, f32[1024]{0:T(1024)S(1)}, ...), condition=%wide.region_8.9_spmd.clone.clone, body=%wide.region_1.8_spmd.clone.clone.sunk | while | flops 829438464 | bytes 24546592 | solution.py:139
  108.8 2.7 convolution_add_fusion.2
  113.4 6.3 %conditional.4 = ((f32[1024]{0:T(1024)S(1)}, f32[1024]{0:T(1024)S(1)}, f32[1024,128]{1,0:T(8,128)})) conditional(s32[]{:T(128)} %convert_element_type.129, (f32[1024]{0:T(1024)S(1)}, f32[1024]{0:T(1024)S(1)}, f32[1024,128]{1,0:T(8,128)}) %tuple.70, (s32[]{:T(128)}, s32[]{:T(128)}, bf16[1,1536,256]{2,1,0:T(8,128)(2,1)S(1)}, ...), branch_computations={%region_4.4_spmd, %region_5.7_spmd} | conditional | flops 553914368 | bytes 14516288 | solution.py:113
  116.4 3.3 fusion.13
  123.5 2.7 convolution_add_fusion.2
  132.0 2.7 convolution_add_fusion.2
  140.5 2.7 convolution_add_fusion.2
  145.1 4.9 %fusion.65 = f32[1024,1536]{1,0:T(8,128)} fusion(bf16[128,1536]{1,0:T(8,128)(2,1)} %param.23, f32[1024,128]{1,0:T(8,128)} %get-tuple-element.277, f32[1024]{0:T(1024)S(1)} %get-tuple-element.278), kind=kOutput, calls=%fused_computation.89 | convolution fusion | flops 402915328 | bytes 7213056 | tf_op jit(solution)/shard_map/dot_general | solution.py:144
  152.7 92.0 %reduce-scatter.2.cloned.1.call-done = f32[128,1536]{1,0:T(8,128)} async-done(((f32[1024,1536]{1,0:T(8,128)}), f32[128,1536]{1,0:T(8,128)}) %reduce-scatter.2.cloned.1.call-update) | async-done | bytes 786448 | tf_op jit(solution)/shard_map/reduce_scatter | solution.py:143
  247.8 3.7 reshape.208
  251.5 5.5 %scatter_custom_fusion = bf16[768,1536]{1,0:T(8,128)(2,1)} fusion(s32[512]{0:T(512)S(1)} %bitcast.62, bf16[512,1536]{1,0:T(8,128)(2,1)} %reshape.208, bf16[]{:T(256)} %constant.216.clone.1), kind=kCustom, calls=%fused_computation.76 | custom fusion | bytes 2359808 | tf_op jit(solution)/shard_map/scatter | solution.py:167
  257.1 63.9 %all_to_all.19 = bf16[32,1,24,1536]{3,2,1,0:T(8,128)(2,1)S(1)} all-to-all(bf16[32,1,24,1536]{3,2,1,0:T(8,128)(2,1)} %bitcast.58), channel_id=1, replica_groups=mesh['rep'=8,'seq'=4,'tp'=8] {'seq','tp'}, dimensions={0} | all-to-all | bytes 4718592 | tf_op jit(solution)/shard_map/all_to_all | solution.py:172
  321.0 5.7 %fusion.46 = f32[768,1536]{1,0:T(8,128)S(1)} fusion(bf16[768,1536]{1,0:T(8,128)(2,1)S(1)} %bitcast.60, bf16[1,1536,1536]{2,1,0:T(8,128)(2,1)} %param.26), kind=kOutput, calls=%fused_computation.57 | convolution fusion | flops 3623878656 | bytes 11796480 | tf_op jit(solution)/shard_map/dot_general | solution.py:180
  326.7 3.4 convolution_convert_fusion
  330.0 4.7 %all-to-all-start.2 = ((bf16[32,1,24,1536]{3,2,1,0:T(8,128)(2,1)}), bf16[32,1,24,1536]{3,2,1,0:T(8,128)(2,1)}, u32[]{:S(2)}, u32[]{:S(2)}) async-start(bf16[32,1,24,1536]{3,2,1,0:T(8,128)(2,1)} %bitcast.59), calls=%async_computation.3 | async-start | bytes 4718592 | tf_op jit(solution)/shard_map/all_to_all | solution.py:184
  336.8 53.2 %all-to-all-done.2 = bf16[32,1,24,1536]{3,2,1,0:T(8,128)(2,1)} async-done(((bf16[32,1,24,1536]{3,2,1,0:T(8,128)(2,1)}), bf16[32,1,24,1536]{3,2,1,0:T(8,128)(2,1)}, u32[]{:S(2)}, u32[]{:S(2)}) %all-to-all-start.2) | async-done | bytes 2359328 | tf_op jit(solution)/shard_map/all_to_all | solution.py:184
  390.0 6.4 %gather_fusion = bf16[512,1536]{1,0:T(8,128)(2,1)} fusion(bf16[768,1536]{1,0:T(8,128)(2,1)} %bitcast.14, s32[1024]{0:T(1024)S(1)} %pad_clamp_fusion), kind=kCustom, calls=%fused_computation | custom fusion | bytes 3147776 | tf_op jit(solution)/shard_map/gather | solution.py:187
  396.4 4.2 %reshape.195 = f32[128,4,1536]{2,1,0:T(4,128)} reshape(bf16[512,1536]{1,0:T(8,128)(2,1)} %gather_fusion) | data formatting | bytes 4718592 | tf_op jit(solution)/shard_map/convert_element_type | solution.py:188
  400.6 4.2 %multiply_reduce_fusion = f32[128,1536]{1,0:T(8,128)S(1)} fusion(f32[128,4,1536]{2,1,0:T(4,128)} %reshape.195, f32[128,4]{1,0:T(8,128)S(1)} %copy.54), kind=kLoop, calls=%fused_computation.60 | loop fusion | flops 1376256 | bytes 3934208 | tf_op jit(solution)/shard_map/reduce_sum | solution.py:188
  (119 shorter events, 45.7 us)
Async XLA Ops:
  7.2 319.5 %copy-start = (bf16[1,768,1536]{2,1,0:T(8,128)(2,1)S(1)}, bf16[1,768,1536]{2,1,0:T(8,128)(2,1)}, u32[]{:S(2)}) copy-start(bf16[1,768,1536]{2,1,0:T(8,128)(2,1)} %param.27) | copy-start | bytes 7077892
  7.2 53.8 %all-gather.2.cloned.1.call-start = ((), (), s32[]{:S(2)}) async-start(), calls=%async_computation.4 | async-start | bytes 3538944 | tf_op jit(solution)/shard_map/all_gather | solution.py:73
  12.2 21.8 %all-to-all-start = ((bf16[8,1,64,256]{3,2,1,0:T(8,128)(2,1)}), bf16[8,1,64,256]{3,2,1,0:T(8,128)(2,1)S(1)}, u32[]{:S(2)}, u32[]{:S(2)}) async-start(bf16[8,1,64,256]{3,2,1,0:T(8,128)(2,1)} %constant_dynamic-slice_fusion.2), calls=%async_computation | async-start | bytes 524288 | tf_op jit(solution)/shard_map/all_to_all | solution.py:81
  23.7 221.1 %reduce-scatter.2.cloned.1.call-start = ((), (), s32[]{:S(2)}) async-start(), calls=%async_computation.5 | async-start | bytes 7077888 | tf_op jit(solution)/shard_map/reduce_scatter | solution.py:143
  34.9 29.5 %copy-start.4 = (bf16[512,256]{0,1:T(8,128)(2,1)S(1)}, bf16[512,256]{0,1:T(8,128)(2,1)}, u32[]{:S(2)}) copy-start(bf16[512,256]{0,1:T(8,128)(2,1)} %copy.48) | copy-start | bytes 786436
  64.3 19.3 %copy-start.5 = (bf16[1024,384]{0,1:T(8,128)(2,1)}, bf16[1024,384]{0,1:T(8,128)(2,1)S(1)}, u32[]{:S(2)}) copy-start(bf16[1024,384]{0,1:T(8,128)(2,1)S(1)} %convolution_convert_fusion.1) | copy-start | bytes 2359300
  64.3 19.4 %copy-start.9 = (s32[8]{0:T(128)S(1)}, s32[8]{0:T(128)}, u32[]{:S(2)}) copy-start(s32[8]{0:T(128)} %param.18) | copy-start | bytes 100
  64.4 19.2 %copy-start.3 = (bf16[1024,256]{0,1:T(8,128)(2,1)}, bf16[1024,256]{0,1:T(8,128)(2,1)S(1)}, u32[]{:S(2)}) copy-start(bf16[1024,256]{0,1:T(8,128)(2,1)S(1)} %slice.74) | copy-start | bytes 1572868
  64.5 19.2 %collective-permute-start = (bf16[1536,256]{0,1:T(8,128)(2,1)S(1)}, bf16[1536,256]{0,1:T(8,128)(2,1)}, u32[]{:S(2)}, u32[]{:S(2)}) collective-permute-start(bf16[1536,256]{0,1:T(8,128)(2,1)S(1)} %pad_maximum_fusion), channel_id=1, source_target_pairs={{0,8},{8,16},{16,24},{24,0},{1,9},{9,17},{17,25},{25,1},{2,10},{10... | collective-permute-start | bytes 2359304 | tf_op jit(solution)/shard_map/ppermute | solution.py:123
  66.1 27.4 %collective-permute-start.1 = (bf16[1536,256]{0,1:T(8,128)(2,1)S(1)}, bf16[1536,256]{0,1:T(8,128)(2,1)}, u32[]{:S(2)}, u32[]{:S(2)}) collective-permute-start(bf16[1536,256]{0,1:T(8,128)(2,1)S(1)} %pad_maximum_fusion), channel_id=1, source_target_pairs={{0,24},{8,0},{16,8},{24,16},{1,25},{9,1},{17,9},{25,17},{2,26},{10... | collective-permute-start | bytes 2359304 | tf_op jit(solution)/shard_map/ppermute | solution.py:128
  83.6 18.1 %collective-permute-start.2 = (bf16[1536,256]{0,1:T(8,128)(2,1)}, bf16[1536,256]{0,1:T(8,128)(2,1)}, u32[]{:S(2)}, u32[]{:S(2)}) collective-permute-start(bf16[1536,256]{0,1:T(8,128)(2,1)} %collective-permute-done), channel_id=1, source_target_pairs={{0,8},{8,16},{16,24},{24,0},{1,9},{9,17},{17,25},{25,1},{2,10},{10... | collective-permute-start | bytes 2359304 | tf_op jit(solution)/shard_map/ppermute | solution.py:123
  88.3 1.9 copy-start.2
  149.9 0.7 copy-start.7
  149.9 94.8 %copy-start.1 = (bf16[128,1536]{1,0:T(8,128)(2,1)S(1)}, bf16[128,1536]{1,0:T(8,128)(2,1)}, u32[]{:S(2)}) copy-start(bf16[128,1536]{1,0:T(8,128)(2,1)} %param.16) | copy-start | bytes 1179652
  149.9 96.2 %copy-start.8 = (f32[1536]{0:T(1024)S(1)}, f32[1536]{0:T(1024)}, u32[]{:S(2)}) copy-start(f32[1536]{0:T(1024)} %param.24) | copy-start | bytes 18436
  330.0 6.3 %copy-start.6 = (bf16[1536,32]{0,1:T(8,128)(2,1)S(1)}, bf16[1536,32]{0,1:T(8,128)(2,1)}, u32[]{:S(2)}) copy-start(bf16[1536,32]{0,1:T(8,128)(2,1)} %param.25) | copy-start | bytes 294916
  330.0 60.0 %all-to-all-start.2 = ((bf16[32,1,24,1536]{3,2,1,0:T(8,128)(2,1)}), bf16[32,1,24,1536]{3,2,1,0:T(8,128)(2,1)}, u32[]{:S(2)}, u32[]{:S(2)}) async-start(bf16[32,1,24,1536]{3,2,1,0:T(8,128)(2,1)} %bitcast.59), calls=%async_computation.3 | async-start | bytes 4718592 | tf_op jit(solution)/shard_map/all_to_all | solution.py:184
Sparse Core Ops, SparseCore 0:
  10.6 50.3 all-gather.1
  150.1 94.6 reduce-scatter.1
